TPU v7x, 256 devices: a whole 4x4x8 slice. The times are simulated.
256 devices in a mesh: leaf: 16 (over z, core), group: 16 (over x, y).
Axes of the slice: x: 4, y: 4, z: 8, core: 2. Of those that a mesh axis runs over, the one named last changes fastest.
Arguments:
- tile_fields: bfloat16 [2048, 32, 32, 512], P(('leaf', 'group')), may hold values from -2500 to 2500
- routes: int32 [256, 8], P(('leaf', 'group')), may hold values from 0 to 15, as said below
- counts: int32 [256], P(('leaf', 'group')), may hold values from 5 to 8
Outputs:
- factor: float32 [16, 16], replicated
- mode_blocks: float32 [4096, 256, 256], P(('leaf', 'group'))
Inputs may be any that keep to these rules, and one draw needn't show every extreme that they name: `routes`: the 8 entries of a device are distinct. In every group some leaf index is named by an occupied slot of every device of the group, and every leaf index is named by an occupied slot of some device of the group.
All inputs are finite; a program needn't handle non-finite values.
Results may differ from a plain program's by a relative error of at most 0.012.
The roundings to bfloat16 on the way count: a program that leaves them out, or rounds other values in their place, can miss the bound.
Values may be sent and summed in bfloat16 or wider, within the bound.
A program may use at most 128 MiB of HBM per device.

v0:
```python
import jax
import jax.numpy as jnp
from jax import lax
from jax.sharding import PartitionSpec as P


def smoother(length):
    half_edge = length // 2
    row_index = jnp.arange(half_edge)[:, None]
    col_index = jnp.arange(length)[None, :]
    offset = (col_index - 2 * row_index).astype(jnp.float32)
    tap_offsets = jnp.arange(-4, 5).astype(jnp.float32)
    normalizer = jnp.sum(jnp.exp(-tap_offsets * tap_offsets / 4.5))
    weights = jnp.where(jnp.abs(offset) <= 4.0, jnp.exp(-offset * offset / 4.5) / normalizer, 0.0)
    return weights.astype(jnp.bfloat16)


def cholesky_upper(gram):
    order = gram.shape[0]
    positions = jnp.arange(order)
    upper = jnp.zeros_like(gram)
    for row_index in range(order):
        partial_row = gram[row_index] - jnp.sum(upper[:, row_index][:, None] * upper, axis=0)
        pivot = jnp.sqrt(partial_row[row_index])
        new_row = jnp.where(
            positions >= row_index, partial_row / pivot, jnp.zeros_like(partial_row)
        )
        upper = upper.at[row_index].set(new_row)
    return upper


def invert_upper(upper):
    order = upper.shape[0]
    positions = jnp.arange(order)
    identity = jnp.eye(order, dtype=upper.dtype)
    result = jnp.zeros_like(upper)
    for row_index in range(order - 1, -1, -1):
        off_diagonal = jnp.where(
            positions > row_index, upper[row_index], jnp.zeros_like(upper[row_index])
        )
        partial_row = identity[row_index] - jnp.sum(off_diagonal[:, None] * result, axis=0)
        result = result.at[row_index].set(partial_row / upper[row_index, row_index])
    return result


def filter_tiles(payload):
    slots_here = payload.shape[0]
    tile_edge = payload.shape[1]
    half_edge = tile_edge // 2
    snapshots = payload.shape[3] // tile_edge
    weights = smoother(tile_edge)
    first_pass = jnp.einsum(
        "ix,sxr->sir",
        weights,
        payload.reshape(slots_here, tile_edge, tile_edge * tile_edge * snapshots),
        preferred_element_type=jnp.float32,
    ).astype(jnp.bfloat16)
    second_pass = jnp.einsum(
        "jy,siyc->sijc",
        weights,
        first_pass.reshape(slots_here, half_edge, tile_edge, tile_edge * snapshots),
        preferred_element_type=jnp.float32,
    ).astype(jnp.bfloat16)
    depth_table = jnp.kron(weights, jnp.eye(snapshots, dtype=jnp.bfloat16))
    flat_second = second_pass.reshape(slots_here * half_edge * half_edge, tile_edge * snapshots)
    third_pass = lax.dot_general(
        flat_second, depth_table, (((1,), (1,)), ((), ())), preferred_element_type=jnp.float32
    ).astype(jnp.bfloat16)
    return third_pass.reshape(slots_here, half_edge * half_edge, half_edge * snapshots)


def gram_matrix(filtered, snapshots):
    flat_rows = filtered.reshape(-1, filtered.shape[-1] // snapshots, snapshots)
    return lax.dot_general(
        flat_rows, flat_rows, (((0, 1), (0, 1)), ((), ())), preferred_element_type=jnp.float32
    )


def place_tiles(payload, route_row, count_here, leaves):
    buffer = jnp.zeros((leaves,) + payload.shape[1:], payload.dtype)
    for slot_index in range(payload.shape[0]):
        tile_piece = jnp.where(
            slot_index < count_here, payload[slot_index], jnp.zeros_like(payload[slot_index])
        )
        buffer = lax.dynamic_update_slice_in_dim(buffer, tile_piece[None], route_row[slot_index], 0)
    return buffer


def shards(tile_fields, routes, counts):
    leaves = lax.axis_size("leaf")
    groups = lax.axis_size("group")
    slots_here = tile_fields.shape[0]
    tile_edge = tile_fields.shape[1]
    snapshots = tile_fields.shape[3] // tile_edge
    half_edge = tile_edge // 2
    rows_all = half_edge**3 * slots_here * leaves * groups
    route_row = routes[0]
    count_here = counts[0]
    incoming = lax.all_to_all(
        place_tiles(tile_fields, route_row, count_here, leaves),
        "leaf",
        split_axis=0,
        concat_axis=0,
        tiled=True,
    )
    arrived = filter_tiles(incoming)
    local_gram = gram_matrix(arrived, snapshots)
    summed = lax.psum(local_gram, ("leaf", "group"))
    factor = cholesky_upper(summed / rows_all)
    inverse = invert_upper(factor)
    block_inverse = jnp.kron(jnp.eye(half_edge, dtype=jnp.float32), inverse)
    flat_rows = arrived.reshape(leaves * half_edge * half_edge, half_edge * snapshots).astype(
        jnp.float32
    )
    mode_blocks = jnp.dot(flat_rows, block_inverse, precision=lax.Precision.HIGHEST)
    return (factor, mode_blocks.reshape(leaves, half_edge * half_edge, half_edge * snapshots))


def solution(mesh):
    return jax.shard_map(
        shards,
        mesh=mesh,
        in_specs=(
            P(("leaf", "group"), None, None, None),
            P(("leaf", "group"), None),
            P(("leaf", "group")),
        ),
        out_specs=(P(), P(("leaf", "group"), None, None)),
        check_vma=False,
    )
```

profile of v0, /device:TPU:1, one launch (start us, length us, event | category | flops | bytes accessed | tf_op | source)
XLA Modules:
  0.0 622.5 jit_solution(9531453409262674630)
XLA Ops:
  0.6 1.6 fusion.44
  18.1 8.0 %broadcast_in_dim.9 = bf16[16,32,32,512]{3,2,1,0:T(8,128)(2,1)} broadcast(bf16[]{:T(256)} %constant.803.clone.1), dimensions={} | broadcast | bytes 16777218 | tf_op jit(solution)/shard_map/broadcast_in_dim | solution.py:80
  36.2 10.0 %all-to-all-start = ((bf16[16,32,32,512]{3,2,1,0:T(8,128)(2,1)}), bf16[16,32,32,512]{3,2,1,0:T(8,128)(2,1)}, u32[]{:S(2)}, u32[]{:S(2)}) async-start(bf16[16,32,32,512]{3,2,1,0:T(8,128)(2,1)} %select_dynamic-update-slice_fusion), calls=%async_computation | async-start | bytes 33554432 | tf_op jit(solution)/shard_map/all_to_all | solution.py:99
  47.8 3.6 mul.363
  51.4 357.9 %all-to-all-done = bf16[16,32,32,512]{3,2,1,0:T(8,128)(2,1)} async-done(((bf16[16,32,32,512]{3,2,1,0:T(8,128)(2,1)}), bf16[16,32,32,512]{3,2,1,0:T(8,128)(2,1)}, u32[]{:S(2)}, u32[]{:S(2)}) %all-to-all-start) | async-done | bytes 16777248 | tf_op jit(solution)/shard_map/all_to_all | solution.py:99
  409.3 25.6 %reshape.1109 = bf16[16,32,16384]{2,1,0:T(8,128)(2,1)} reshape(bf16[16,32,32,512]{3,2,1,0:T(8,128)(2,1)} %all-to-all-done) | data formatting | bytes 33554432 | tf_op jit(solution)/shard_map/reshape | solution.py:55
  434.9 12.1 %convolution_convert_fusion = bf16[16,16384,16]{1,2,0:T(8,128)(2,1)} fusion(bf16[16,32,16384]{2,1,0:T(8,128)(2,1)} %reshape.1109, f32[]{:T(128)} %fusion.18, s32[16]{0:T(128)S(1)} %iota_multiply_fusion), kind=kOutput, calls=%fused_computation | convolution fusion | flops 272634880 | bytes 25165892 | tf_op jit(solution)/shard_map/ix,sxr->sir/dot_general | solution.py:52
  446.9 10.4 %copy.9 = bf16[32,8,32,512]{3,2,1,0:T(8,128)(2,1)} copy(bf16[32,8,32,512]{3,1,2,0:T(8,128)(2,1)} %bitcast.268) | data formatting | bytes 16777216
  457.3 5.3 fusion.2
  462.6 2.6 convolution_convert_fusion.1
  465.3 2.9 copy.7
  469.2 78.0 %psum.7 = f32[16,16]{1,0:T(8,128)S(1)} all-reduce(f32[16,16]{1,0:T(8,128)S(1)} %convolution_bitcast_fusion), channel_id=1, replica_groups=mesh['leaf'=16,'group'=16] {'leaf','group'}, use_global_device_ids=true, to_apply=%region_1.2 | all-reduce | flops 256 | bytes 2048 | tf_op jit(solution)/shard_map/psum | solution.py:108
  595.3 1.3 fusion.33
  596.7 1.3 fusion.32
  599.5 1.4 fusion.30
  601.0 1.4 fusion.29
  602.5 1.3 fusion.28
  603.9 1.3 fusion.27
  605.3 1.4 fusion.26
  606.8 1.4 fusion.25
  609.7 1.3 fusion.23
  611.1 1.3 fusion.22
  613.9 1.3 fusion.20
  617.1 5.4 fusion.45
  (157 shorter events, 57.1 us)
Async XLA Ops:
  18.1 8.4 %copy-start = (bf16[8,32,32,512]{3,2,1,0:T(8,128)(2,1)S(1)}, bf16[8,32,32,512]{3,2,1,0:T(8,128)(2,1)}, u32[]{:S(2)}) copy-start(bf16[8,32,32,512]{3,2,1,0:T(8,128)(2,1)} %param.67) | copy-start | bytes 25165828
  36.2 373.1 %all-to-all-start = ((bf16[16,32,32,512]{3,2,1,0:T(8,128)(2,1)}), bf16[16,32,32,512]{3,2,1,0:T(8,128)(2,1)}, u32[]{:S(2)}, u32[]{:S(2)}) async-start(bf16[16,32,32,512]{3,2,1,0:T(8,128)(2,1)} %select_dynamic-update-slice_fusion), calls=%async_computation | async-start | bytes 33554432 | tf_op jit(solution)/shard_map/all_to_all | solution.py:99
  51.4 543.2 %copy-start.2 = (f32[16,16]{1,0:T(8,128)}, f32[16,16]{1,0:T(8,128)S(1)}, u32[]{:S(2)}) copy-start(f32[16,16]{1,0:T(8,128)S(1)} %fusion.9) | copy-start | bytes 3076
  547.2 3.1 copy-start.3
  592.5 30.0 %copy-start.1 = (f32[16,16]{1,0:T(8,128)}, f32[16,16]{1,0:T(8,128)S(1)}, u32[]{:S(2)}) copy-start(f32[16,16]{1,0:T(8,128)S(1)} %scatter.131) | copy-start | bytes 3076
where the time goes:
time: 626 us; the launch traced here: 623 us
  waiting for transfers between devices  358 us (57%)
  blocking collectives  78 us (12%)
  local copies, waits for them, and re-layouts  67.7 us (11%)
  other arithmetic  55.3 us (9%)
  between operations  27.2 us (4%)
  matrix products  26.4 us (4%)
  starting transfers between devices  9.99 us (2%)
    all_to_all x1, waiting for transfers between devices, shards(): lax.all_to_all(place_tiles(tile_fields, route_row, count_here, leaves), '...  358 us
    psum x1, blocking collectives, shards(): summed = lax.psum(local_gram, ('leaf', 'group'))  78 us
    reshape x1, local copies, waits for them, and re-layouts, filter_tiles(): payload.reshape(slots_here, tile_edge, tile_edge * tile_edge * snapshots)  25.6 us
    div x16, other arithmetic, invert_upper(): result = result.at[row_index].set(partial_row / upper[row_index, row_index])  20.2 us
  transfers between devices with their start and end apart: 1, of which 1 were waited for; matrix products, arithmetic and copies ran while one was open for 1% of the time, Pallas kernels for 0%

commit v1 on v0

--- a/solution.py
+++ b/solution.py
@@ -2,6 +2,12 @@
 import jax.numpy as jnp
 from jax import lax
 from jax.sharding import PartitionSpec as P
+
+
+def summed_here(x, mesh_axis):
+    pieces = lax.all_gather(x, mesh_axis, axis=0, tiled=False)
+    summed = pieces.sum(axis=0)
+    return summed
 
 
 def smoother(length):
@@ -105,7 +111,7 @@
     )
     arrived = filter_tiles(incoming)
     local_gram = gram_matrix(arrived, snapshots)
-    summed = lax.psum(local_gram, ("leaf", "group"))
+    summed = summed_here(local_gram, ("leaf", "group"))
     factor = cholesky_upper(summed / rows_all)
     inverse = invert_upper(factor)
     block_inverse = jnp.kron(jnp.eye(half_edge, dtype=jnp.float32), inverse)

time: 626 us -> 682 us (1.089)
  blocking collectives: 78 us -> 129 us
    all_gather x0 -> x1, blocking collectives: none -> 129 us  [summed_here(): pieces = lax.all_gather(x, mesh_axis, axis=0, tiled=False)]
    psum x1 -> x0, blocking collectives: 78 us -> none  [shards(): summed = lax.psum(local_gram, ('leaf', 'group'))]
where the time goes in v1:
time: 682 us; the launch traced here: 679 us
  waiting for transfers between devices  358 us (52%)
  blocking collectives  129 us (19%)
  local copies, waits for them, and re-layouts  70.2 us (10%)
  other arithmetic  58.5 us (9%)
  between operations  28.3 us (4%)
  matrix products  24.8 us (4%)
  starting transfers between devices  9.99 us (1%)
    all_to_all x1, waiting for transfers between devices, shards(): lax.all_to_all(place_tiles(tile_fields, route_row, count_here, leaves), '...  358 us
    all_gather x1, blocking collectives, summed_here(): pieces = lax.all_gather(x, mesh_axis, axis=0, tiled=False)  129 us
    reshape x1, local copies, waits for them, and re-layouts, filter_tiles(): payload.reshape(slots_here, tile_edge, tile_edge * tile_edge * snapshots)  25.6 us
    div x16, other arithmetic, invert_upper(): result = result.at[row_index].set(partial_row / upper[row_index, row_index])  20.1 us
  transfers between devices with their start and end apart: 1, of which 1 were waited for; matrix products, arithmetic and copies ran while one was open for 1% of the time, Pallas kernels for 0%

profile of v1, /device:TPU:1, one launch (start us, length us, event | category | flops | bytes accessed | tf_op | source)
XLA Modules:
  0.0 678.5 jit_solution(9352670388414848968)
XLA Ops:
  0.6 1.6 fusion.44
  18.1 8.0 %broadcast_in_dim.9 = bf16[16,32,32,512]{3,2,1,0:T(8,128)(2,1)} broadcast(bf16[]{:T(256)} %constant.803.clone.1), dimensions={} | broadcast | bytes 16777218 | tf_op jit(solution)/shard_map/broadcast_in_dim | solution.py:86
  36.2 10.0 %all-to-all-start = ((bf16[16,32,32,512]{3,2,1,0:T(8,128)(2,1)}), bf16[16,32,32,512]{3,2,1,0:T(8,128)(2,1)}, u32[]{:S(2)}, u32[]{:S(2)}) async-start(bf16[16,32,32,512]{3,2,1,0:T(8,128)(2,1)} %select_dynamic-update-slice_fusion), calls=%async_computation | async-start | bytes 33554432 | tf_op jit(solution)/shard_map/all_to_all | solution.py:105
  47.8 3.6 mul.363
  51.4 357.9 %all-to-all-done = bf16[16,32,32,512]{3,2,1,0:T(8,128)(2,1)} async-done(((bf16[16,32,32,512]{3,2,1,0:T(8,128)(2,1)}), bf16[16,32,32,512]{3,2,1,0:T(8,128)(2,1)}, u32[]{:S(2)}, u32[]{:S(2)}) %all-to-all-start) | async-done | bytes 16777248 | tf_op jit(solution)/shard_map/all_to_all | solution.py:105
  409.3 25.6 %reshape.1109 = bf16[16,32,16384]{2,1,0:T(8,128)(2,1)} reshape(bf16[16,32,32,512]{3,2,1,0:T(8,128)(2,1)} %all-to-all-done) | data formatting | bytes 33554432 | tf_op jit(solution)/shard_map/reshape | solution.py:61
  434.9 12.1 %convolution_convert_fusion = bf16[16,16384,16]{1,2,0:T(8,128)(2,1)} fusion(bf16[16,32,16384]{2,1,0:T(8,128)(2,1)} %reshape.1109, f32[]{:T(128)} %fusion.18, s32[16]{0:T(128)S(1)} %iota_multiply_fusion), kind=kOutput, calls=%fused_computation | convolution fusion | flops 272634880 | bytes 25165892 | tf_op jit(solution)/shard_map/ix,sxr->sir/dot_general | solution.py:58
  446.9 10.4 %copy.9 = bf16[32,8,32,512]{3,2,1,0:T(8,128)(2,1)} copy(bf16[32,8,32,512]{3,1,2,0:T(8,128)(2,1)} %bitcast.269) | data formatting | bytes 16777216
  457.3 5.3 fusion.2
  462.6 2.6 convolution_convert_fusion.1
  465.3 2.9 copy.7
  469.1 128.9 %all-gather = f32[4096,16]{1,0:T(8,128)} all-gather(f32[16,16]{1,0:T(8,128)S(1)} %convolution_bitcast_fusion), channel_id=2, replica_groups=mesh['leaf'=16,'group'=16] {'leaf','group'}, dimensions={0}, use_global_device_ids=true | all-gather | bytes 263168 | tf_op jit(solution)/shard_map/all_gather | solution.py:8
  598.0 1.9 reduce_sum.368
  650.2 1.3 fusion.33
  653.0 1.3 fusion.31
  655.9 1.3 fusion.29
  657.3 1.3 fusion.28
  658.7 1.4 fusion.27
  661.5 1.4 fusion.25
  667.2 1.3 fusion.21
  668.6 1.3 fusion.20
  670.0 2.3 broadcast_multiply_fusion
  672.2 2.4 reshape.1116
  674.7 3.8 fusion.45
  (160 shorter events, 60.4 us)
Async XLA Ops:
  18.1 8.4 %copy-start.1 = (bf16[8,32,32,512]{3,2,1,0:T(8,128)(2,1)S(1)}, bf16[8,32,32,512]{3,2,1,0:T(8,128)(2,1)}, u32[]{:S(2)}) copy-start(bf16[8,32,32,512]{3,2,1,0:T(8,128)(2,1)} %param.67) | copy-start | bytes 25165828
  36.2 373.1 %all-to-all-start = ((bf16[16,32,32,512]{3,2,1,0:T(8,128)(2,1)}), bf16[16,32,32,512]{3,2,1,0:T(8,128)(2,1)}, u32[]{:S(2)}, u32[]{:S(2)}) async-start(bf16[16,32,32,512]{3,2,1,0:T(8,128)(2,1)} %select_dynamic-update-slice_fusion), calls=%async_computation | async-start | bytes 33554432 | tf_op jit(solution)/shard_map/all_to_all | solution.py:105
  51.4 598.1 %copy-start.3 = (f32[16,16]{1,0:T(8,128)}, f32[16,16]{1,0:T(8,128)S(1)}, u32[]{:S(2)}) copy-start(f32[16,16]{1,0:T(8,128)S(1)} %fusion.9) | copy-start | bytes 3076
  469.1 205.5 %copy-start = (bf16[4096,256]{1,0:T(8,128)(2,1)S(1)}, bf16[4096,256]{1,0:T(8,128)(2,1)}, u32[]{:S(2)}) copy-start(bf16[4096,256]{1,0:T(8,128)(2,1)} %convolution_convert_fusion.1) | copy-start | bytes 6291460
  599.9 3.4 copy-start.4
  647.4 31.2 %copy-start.2 = (f32[16,16]{1,0:T(8,128)}, f32[16,16]{1,0:T(8,128)S(1)}, u32[]{:S(2)}) copy-start(f32[16,16]{1,0:T(8,128)S(1)} %scatter.131) | copy-start | bytes 3076
